TPU v7x, 32 devices: a whole 2x2x4 slice. The times are simulated.
32 devices in a mesh: col: 16 (over z, x, core), row: 2 (over y).
Axes of the slice: x: 2, y: 2, z: 4, core: 2. Of those that a mesh axis runs over, the one named last changes fastest.
Arguments:
- uniq_rows: bfloat16 [32, 128, 1536], P('row', 'col'), may hold values from -6 to 6
- row_ids: int32 [32, 128, 8], P('row', 'col'), may hold values from 0 to 255, as said below
- sample_idx: int32 [512, 128], P('row', 'col'), may hold values from 0 to 7, as said below
- fm_proj: bfloat16 [128, 8], replicated, may hold values from -0.5 to 0.5
- ln_gain: float32 [1024], replicated, may hold values from 0.5 to 1.5
- w_up: bfloat16 [1024, 2048], P(None, 'row'), may hold values from -0.1875 to 0.1875
- w_down: bfloat16 [2048, 1536], P('row'), may hold values from -0.125 to 0.125
- w_lc: bfloat16 [8, 128], replicated, may hold values from -0.5 to 0.5
- w_res: bfloat16 [16, 128], replicated, may hold values from -0.5 to 0.5
- out_gain: float32 [192], replicated, may hold values from 0.5 to 1.5
- cotangent: bfloat16 [512, 3072], P(('row', 'col')), may hold values from -6 to 6
- moment1: float32 [128, 256, 192], P('col', 'row'), may hold values from -1.5 to 1.5
- moment2: float32 [128, 256], P('col', 'row'), may hold values from 0.01 to 0.1
Outputs:
- layer_out: bfloat16 [512, 3072], P(('row', 'col'))
- new_moment1: float32 [128, 256, 192], P('col', 'row')
- new_moment2: float32 [128, 256], P('col', 'row')
- row_step: float32 [128, 256, 192], P('col', 'row')
Inputs may be any that keep to these rules, and one draw needn't show every extreme that they name: `sample_idx`: for each block of 16 samples and each slot, every one of the 8 list entries is used by at least one sample of the block. `row_ids`: the 8 ids of one list are distinct. Row v of a slot is owned by index v // 128 of row. Of the 1024 list entries held by one device (the blocks of its index of row, the slots of its index of col), at most 640 name rows of one owner, and in every draw some owner is named exactly 640 times on each device.
All inputs are finite; a program needn't handle non-finite values.
Results may differ from a plain program's by a relative error of at most 0.005.
Values may be sent and summed in bfloat16 or wider, within the bound.
A program may use at most 64 MiB of HBM per device.

v0:
```python
import jax
import jax.numpy as jnp
from jax import lax
from jax.sharding import PartitionSpec as P

HIGH = lax.Precision.HIGHEST


def layer_norm(values, gain):
    centered = values - jnp.mean(values, -1, keepdims=True)
    inverse = lax.rsqrt(jnp.mean(centered * centered, -1, keepdims=True) + 1e-05)
    normed = centered * inverse
    return (normed * gain, normed, inverse)


def norm_back(grad_out, normed, inverse):
    first = jnp.mean(grad_out, -1, keepdims=True)
    second = jnp.mean(grad_out * normed, -1, keepdims=True)
    return (grad_out - first - normed * second) * inverse


def silu_grad(values):
    sigma = jax.nn.sigmoid(values)
    return sigma * (1.0 + values * (1.0 - sigma))


def body(
    uniq_rows,
    row_ids,
    sample_idx,
    fm_proj,
    ln_gain,
    w_up,
    w_down,
    w_lc,
    w_res,
    out_gain,
    cotangent,
    moment1,
    moment2,
):
    columns = lax.axis_size("col")
    owners = lax.axis_size("row")
    slot_dev = uniq_rows.shape[1]
    width = out_gain.shape[0]
    uniq = uniq_rows.shape[2] // width
    samples = cotangent.shape[0]
    slots = slot_dev * columns
    vocab_dev = moment2.shape[1]
    rank = fm_proj.shape[1]
    fm_rows = w_down.shape[1] // width
    out_rows = w_res.shape[0]
    entry_iota = jnp.arange(uniq, dtype=jnp.int32)
    index_local = sample_idx.reshape(columns, samples, slot_dev)
    index = lax.all_to_all(index_local, "col", split_axis=0, concat_axis=2, tiled=True).reshape(
        samples, slots
    )
    picker = (index[:, :, None] == entry_iota).astype(jnp.bfloat16)
    moved = lax.all_to_all(uniq_rows, "col", split_axis=0, concat_axis=1, tiled=True)
    table = moved.reshape(slots, uniq, width)
    embed = jnp.einsum("stl,tle->ste", picker, table, preferred_element_type=jnp.float32).astype(
        jnp.bfloat16
    )
    compress = jnp.einsum("ste,tk->sek", embed, fm_proj, preferred_element_type=jnp.float32).astype(
        jnp.bfloat16
    )
    gram = jnp.einsum("ste,sek->stk", embed, compress, preferred_element_type=jnp.float32)
    flat = gram.reshape(samples, slots * rank)
    scaled, normed_in, inverse_in = layer_norm(flat, ln_gain)
    normal_in = scaled.astype(jnp.bfloat16)
    hidden_pre = jnp.dot(
        lax.all_gather(normal_in, "row", axis=0, tiled=True),
        w_up,
        preferred_element_type=jnp.float32,
    )
    hidden = jax.nn.silu(hidden_pre).astype(jnp.bfloat16)
    part_rows = hidden
    fm_out = lax.psum_scatter(
        jnp.dot(part_rows, w_down, preferred_element_type=jnp.float32),
        "row",
        scatter_dimension=0,
        tiled=True,
    )
    linear = jnp.einsum("lt,ste->sle", w_lc, embed, preferred_element_type=jnp.float32)
    joined = jnp.concatenate([fm_out.reshape(samples, fm_rows, width), linear], 1)
    normed_out, normed_rows, inverse_rows = layer_norm(joined, out_gain)
    residual = jnp.einsum("ot,ste->soe", w_res, embed, preferred_element_type=jnp.float32)
    layer_out = (normed_out + residual).reshape(samples, out_rows * width).astype(jnp.bfloat16)
    upstream = cotangent.astype(jnp.float32).reshape(samples, out_rows, width)
    grad_joined = norm_back(upstream * out_gain, normed_rows, inverse_rows)
    grad_fm = grad_joined[:, :fm_rows].reshape(samples, fm_rows * width).astype(jnp.bfloat16)
    grad_hidden = lax.dot_general(
        lax.all_gather(grad_fm, "row", axis=0, tiled=True),
        w_down,
        (((1,), (1,)), ((), ())),
        preferred_element_type=jnp.float32,
    )
    grad_pre = (grad_hidden * silu_grad(hidden_pre)).astype(jnp.bfloat16)
    part_rows = grad_pre
    grad_flat = lax.psum_scatter(
        lax.dot_general(
            part_rows, w_up, (((1,), (1,)), ((), ())), preferred_element_type=jnp.float32
        ).astype(jnp.bfloat16),
        "row",
        scatter_dimension=0,
        tiled=True,
    ).astype(jnp.float32)
    grad_gram = norm_back(grad_flat * ln_gain, normed_in, inverse_in).reshape(samples, slots, rank)
    grad_embed = jnp.einsum("stk,sek->ste", grad_gram, compress.astype(jnp.float32), precision=HIGH)
    grad_comp = jnp.einsum(
        "ste,stk->sek", embed, grad_gram, precision=HIGH, preferred_element_type=jnp.float32
    )
    grad_embed = grad_embed + jnp.einsum(
        "tk,sek->ste", fm_proj.astype(jnp.float32), grad_comp, precision=HIGH
    )
    grad_embed = grad_embed + jnp.einsum(
        "lt,sle->ste", w_lc.astype(jnp.float32), grad_joined[:, fm_rows:], precision=HIGH
    )
    grad_embed = grad_embed + jnp.einsum(
        "ot,soe->ste", w_res.astype(jnp.float32), upstream, precision=HIGH
    )
    list_grads = jnp.einsum("stl,ste->tle", picker.astype(jnp.float32), grad_embed, precision=HIGH)
    returned = lax.all_to_all(
        list_grads.reshape(columns, slot_dev, uniq * width),
        "col",
        split_axis=0,
        concat_axis=0,
        tiled=True,
    )
    entry_grads = returned.reshape(columns * slot_dev * uniq, width)
    row_list = row_ids.reshape(-1)
    slot_of = jnp.broadcast_to(
        jnp.arange(slot_dev, dtype=jnp.int32)[None, :, None], row_ids.shape
    ).reshape(-1)
    owner = row_list // vocab_dev
    target = slot_of * vocab_dev + row_list % vocab_dev
    span = slot_dev * vocab_dev
    entries = row_list.shape[0]
    capacity = 5 * entries // (4 * owners)
    onehot = (owner[:, None] == jnp.arange(owners, dtype=jnp.int32)).astype(jnp.int32)
    before = jnp.cumsum(onehot, 0) - onehot
    place = jnp.sum(before * onehot, 1)
    target_slot = owner * capacity + place
    bucket = jnp.zeros((owners * capacity, width), jnp.float32).at[target_slot].set(entry_grads)
    labels = (
        jnp.full((owners * capacity,), -1.0, jnp.float32)
        .at[target_slot]
        .set(target.astype(jnp.float32))
    )
    got_rows, got_labels = (
        lax.all_to_all(
            bucket.reshape(owners, capacity, width), "row", split_axis=0, concat_axis=0, tiled=True
        ),
        lax.all_to_all(
            labels.reshape(owners, capacity), "row", split_axis=0, concat_axis=0, tiled=True
        ),
    )
    segment = jnp.where(got_labels >= 0.0, got_labels, float(span)).astype(jnp.int32).reshape(-1)
    summed = jax.ops.segment_sum(got_rows.reshape(-1, width), segment, num_segments=span + 1)[:span]
    row_grads = summed.reshape(slot_dev, vocab_dev, width)
    new_moment1 = 0.9 * moment1 + 0.1 * row_grads
    new_moment2 = 0.99 * moment2 + 0.01 * jnp.mean(row_grads * row_grads, -1)
    row_step = new_moment1 * lax.rsqrt(new_moment2)[..., None]
    return (layer_out, new_moment1, new_moment2, row_step)


def solution(mesh):
    return jax.shard_map(
        body,
        mesh=mesh,
        in_specs=(
            P("row", "col", None),
            P("row", "col", None),
            P("row", "col"),
            P(),
            P(),
            P(None, "row"),
            P("row", None),
            P(),
            P(),
            P(),
            P(("row", "col"), None),
            P("col", "row", None),
            P("col", "row"),
        ),
        out_specs=(
            P(("row", "col"), None),
            P("col", "row", None),
            P("col", "row"),
            P("col", "row", None),
        ),
        check_vma=False,
    )
```

profile of v0, /device:TPU:0, one launch (start us, length us, event | category | flops | bytes accessed | tf_op | source)
XLA Modules:
  0.0 204.6 jit_solution(17181912444277728995)
XLA Ops:
  7.2 0.9 reshape.259
  8.2 13.6 %all_to_all.46 = s32[16,1,128]{2,1,0:T(1,128)S(1)} all-to-all(s32[16,1,128]{2,1,0:T(1,128)S(1)} %reshape.316), channel_id=1, replica_groups=mesh['col'=16,'row'=2] {'col'}, dimensions={0} | all-to-all | bytes 16384 | tf_op jit(solution)/shard_map/all_to_all | solution.py:55
  21.9 3.6 %all-to-all-start.1 = ((bf16[16,8,1536]{2,1,0:T(8,128)(2,1)}), bf16[16,8,1536]{2,1,0:T(8,128)(2,1)S(1)}, u32[]{:S(2)}, u32[]{:S(2)}) async-start(bf16[16,8,1536]{2,1,0:T(8,128)(2,1)} %param.13), calls=%async_computation.1 | async-start | bytes 786432 | tf_op jit(solution)/shard_map/all_to_all | solution.py:59
  26.0 0.7 reduce.7
  26.7 0.7 reshape.317
  27.4 1.5 bitcast_bitcast_fusion.1
  28.8 8.7 %all-to-all-done.1 = bf16[16,8,1536]{2,1,0:T(8,128)(2,1)S(1)} async-done(((bf16[16,8,1536]{2,1,0:T(8,128)(2,1)}), bf16[16,8,1536]{2,1,0:T(8,128)(2,1)S(1)}, u32[]{:S(2)}, u32[]{:S(2)}) %all-to-all-start.1) | async-done | bytes 393248 | tf_op jit(solution)/shard_map/all_to_all | solution.py:59
  37.5 1.2 reshape.260
  38.8 2.6 %fusion = bf16[16,128,192]{2,0,1:T(8,128)(2,1)} fusion(bf16[128,8,192]{2,1,0:T(8,128)(2,1)} %reshape.260, s32[16,128]{0,1:T(8,128)} %bitcast_bitcast_fusion.1), kind=kOutput, calls=%fused_computation.7 | convolution fusion | flops 6701056 | bytes 1187840 | tf_op jit(solution)/shard_map/stl,tle->ste/dot_general | solution.py:61
  41.4 2.6 %copy.98 = bf16[16,128,192]{1,2,0:T(8,128)(2,1)} copy(bf16[16,128,192]{2,0,1:T(8,128)(2,1)} %fusion) | data formatting | bytes 1572864 | tf_op jit(solution)/shard_map/convert_element_type | solution.py:61
  44.0 1.6 convolution_convert_fusion.1
  45.6 0.7 copy-done.7
  46.3 1.5 fusion.47
  47.8 1.0 copy.99
  49.1 1.2 copy.100
  50.4 4.6 %all_gather.6 = bf16[32,1024]{1,0:T(8,128)(2,1)S(1)} all-gather(bf16[16,1024]{1,0:T(8,128)(2,1)S(1)} %multiply_convert_fusion.2), channel_id=1, replica_groups=mesh['col'=16,'row'=2] {'row'}, dimensions={0}, use_global_device_ids=true | all-gather | bytes 98304 | tf_op jit(solution)/shard_map/all_gather | solution.py:72
  55.0 2.1 %fusion.48 = f32[32,1024]{1,0:T(8,128)S(1)} fusion(bf16[32,1024]{1,0:T(8,128)(2,1)S(1)} %all_gather.6, bf16[1024,1024]{1,0:T(8,128)(2,1)} %param.18), kind=kOutput, calls=%fused_computation.114 | convolution fusion | flops 67108864 | bytes 2293760 | tf_op jit(solution)/shard_map/dot_general | solution.py:71
  57.1 0.6 copy-done.2
  57.7 1.3 fusion.19
  59.3 1.6 convolution_bitcast_fusion.1
  60.9 8.0 %reduce-scatter.3.cloned.1.call-done = f32[16,1536]{1,0:T(8,128)} async-done(((f32[32,1536]{1,0:T(8,128)}), f32[16,1536]{1,0:T(8,128)}) %reduce-scatter.3.cloned.1.call-update) | async-done | bytes 98320 | tf_op jit(solution)/shard_map/reduce_scatter | solution.py:78
  68.9 1.0 reshape.262
  70.2 0.9 fusion.9
  71.2 0.9 subtract_multiply_fusion
  72.1 0.7 copy-done.4
  72.8 0.6 slice.29
  73.4 1.6 convert_element_type.72
  75.0 5.1 %all_gather.7 = bf16[32,1536]{1,0:T(8,128)(2,1)} all-gather(bf16[16,1536]{1,0:T(8,128)(2,1)} %convert_element_type.72), channel_id=1, replica_groups=mesh['col'=16,'row'=2] {'row'}, dimensions={0}, use_global_device_ids=true | all-gather | bytes 147456 | tf_op jit(solution)/shard_map/all_gather | solution.py:93
  80.0 4.0 %convolution_convert_fusion.2 = bf16[32,1024]{1,0:T(8,128)(2,1)} fusion(bf16[1024,1024]{1,0:T(8,128)(2,1)} %param.18, bf16[32,1536]{1,0:T(8,128)(2,1)} %all_gather.7, bf16[1024,1536]{1,0:T(8,128)(2,1)S(1)} %copy-done, f32[32,1024]{1,0:T(8,128)} %copy-done.2), kind=kOutput, calls=%fused_computation.15 | convolution fusion | flops 168099840 | bytes 5537792 | tf_op jit(solution)/shard_map/dot_general | solution.py:101
  84.1 3.5 %fusion.12 = f32[16,192,128]{2,1,0:T(8,128)} fusion(f32[16,16,192]{2,1,0:T(8,128)} %copy-done.4, bf16[8,128]{1,0:T(8,128)(2,1)} %param.20), kind=kOutput, calls=%fused_computation.36 | convolution fusion | flops 37748736 | bytes 1705984 | tf_op jit(solution)/shard_map/lt,sle->ste/dot_general | solution.py:116
  87.6 7.5 %reduce-scatter.5.cloned.1.call-done = bf16[16,1024]{1,0:T(8,128)(2,1)} async-done(((bf16[32,1024]{1,0:T(8,128)(2,1)}), bf16[16,1024]{1,0:T(8,128)(2,1)}) %reduce-scatter.5.cloned.1.call-update) | async-done | bytes 32784 | tf_op jit(solution)/shard_map/reduce_scatter | solution.py:100
  95.1 1.0 fusion.20
  96.2 1.6 subtract_multiply_fusion.2
  97.7 1.8 copy.107
  99.6 1.8 copy.108
  101.4 2.4 %fusion.50 = f32[16,192,8]{1,2,0:T(8,128)S(1)} fusion(bf16[16,128,192]{1,2,0:T(8,128)(2,1)} %copy.98, f32[16,128,8]{1,2,0:T(8,128)} %copy.108), kind=kOutput, calls=%fused_computation.116 | convolution fusion | flops 37748736 | bytes 950272 | tf_op jit(solution)/shard_map/ste,stk->sek/dot_general | solution.py:110
  103.8 1.9 fusion.49
  105.7 1.4 fusion.41
  107.2 1.6 bitcast_add_fusion
  108.8 3.0 %copy.111 = f32[16,128,192]{2,0,1:T(8,128)} copy(f32[16,128,192]{1,2,0:T(8,128)} %bitcast_add_fusion) | data formatting | bytes 3145728 | tf_op jit(solution)/shard_map/add | solution.py:119
  111.8 3.5 %fusion.8 = f32[128,8,192]{2,1,0:T(8,128)} fusion(f32[16,128,192]{2,0,1:T(8,128)} %copy.111, s32[16,128]{0,1:T(8,128)S(1)} %copy-done.6), kind=kOutput, calls=%fused_computation.25 | convolution fusion | flops 37765120 | bytes 2367488 | tf_op jit(solution)/shard_map/stl,ste->tle/dot_general | solution.py:122
  115.3 2.4 %reshape.270 = f32[16,8,1536]{2,1,0:T(8,128)} reshape(f32[128,8,192]{2,1,0:T(8,128)} %fusion.8) | data formatting | bytes 1572864 | tf_op jit(solution)/shard_map/reshape | solution.py:124
  117.7 5.8 %all-to-all-start.3 = ((f32[16,8,1536]{2,1,0:T(8,128)}), f32[16,8,1536]{2,1,0:T(8,128)}, u32[]{:S(2)}, u32[]{:S(2)}) async-start(f32[16,8,1536]{2,1,0:T(8,128)} %reshape.270), calls=%async_computation.5 | async-start | bytes 1572864 | tf_op jit(solution)/shard_map/all_to_all | solution.py:123
  124.0 0.6 reduce-window.6
  125.2 4.3 %scatter_custom_fusion = f32[1280]{0:T(1024)S(1)} fusion(s32[1024]{0:T(1024)S(1)} %bitcast.112, f32[1024]{0:T(1024)S(1)} %get-tuple-element.34, f32[]{:T(128)} %constant.65.clone.1), kind=kCustom, calls=%fused_computation.91 | custom fusion | bytes 5124 | tf_op jit(solution)/shard_map/scatter | solution.py:148
  129.6 0.6 all_to_all.36
  130.2 12.1 %all-to-all-done.3 = f32[16,8,1536]{2,1,0:T(8,128)} async-done(((f32[16,8,1536]{2,1,0:T(8,128)}), f32[16,8,1536]{2,1,0:T(8,128)}, u32[]{:S(2)}, u32[]{:S(2)}) %all-to-all-start.3) | async-done | bytes 786464 | tf_op jit(solution)/shard_map/all_to_all | solution.py:123
  142.3 3.2 %all-to-all-start.2 = ((f32[2,1,640]{2,1,0:T(1,128)}), f32[2,1,640]{2,1,0:T(1,128)S(1)}, u32[]{:S(2)}, u32[]{:S(2)}) async-start(f32[2,1,640]{2,1,0:T(1,128)} %all_to_all.36), calls=%async_computation.3 | async-start | bytes 10240 | tf_op jit(solution)/shard_map/all_to_all | solution.py:154
  145.5 2.4 %reshape.286 = f32[1024,192]{1,0:T(8,128)} reshape(f32[16,8,1536]{2,1,0:T(8,128)} %all-to-all-done.3) | data formatting | bytes 1572864 | tf_op jit(solution)/shard_map/reshape | solution.py:130
  148.0 6.4 %scatter_custom_fusion.1 = f32[1280,192]{1,0:T(8,128)} fusion(s32[1024]{0:T(1024)S(1)} %bitcast.113, f32[1024,192]{1,0:T(8,128)} %reshape.286, f32[]{:T(128)} %constant.59.clone.1), kind=kCustom, calls=%fused_computation.20 | custom fusion | bytes 983552 | tf_op jit(solution)/shard_map/scatter | solution.py:144
  154.4 2.7 %copy.112 = f32[2,640,192]{1,2,0:T(8,128)} copy(f32[2,640,192]{2,1,0:T(8,128)} %bitcast.105) | data formatting | bytes 1966080 | tf_op jit(solution)/shard_map/reshape | solution.py:152
  157.0 4.4 %all-to-all-start.4 = ((f32[2,640,192]{1,2,0:T(8,128)}), f32[2,640,192]{1,2,0:T(8,128)}, u32[]{:S(2)}, u32[]{:S(2)}) async-start(f32[2,640,192]{1,2,0:T(8,128)} %copy.112), calls=%async_computation.6 | async-start | bytes 1966080 | tf_op jit(solution)/shard_map/all_to_all | solution.py:151
  161.5 0.6 fusion.28
  162.1 1.7 fusion.2
  163.7 0.8 convert_element_type.67
  164.6 10.7 %all-to-all-done.4 = f32[2,640,192]{1,2,0:T(8,128)} async-done(((f32[2,640,192]{1,2,0:T(8,128)}), f32[2,640,192]{1,2,0:T(8,128)}, u32[]{:S(2)}, u32[]{:S(2)}) %all-to-all-start.4) | async-done | bytes 983072 | tf_op jit(solution)/shard_map/all_to_all | solution.py:151
  175.2 2.7 %copy.118 = f32[2,640,192]{2,1,0:T(8,128)} copy(f32[2,640,192]{1,2,0:T(8,128)} %all-to-all-done.4) | data formatting | bytes 1966080 | tf_op jit(solution)/shard_map/reshape | solution.py:159
  177.9 10.5 %scatter_custom_fusion.2 = f32[1025,192]{1,0:T(8,128)} fusion(s32[1280]{0:T(1024)} %fusion.28, f32[1280,192]{1,0:T(8,128)} %bitcast.108, f32[]{:T(128)} %constant.59.clone.1), kind=kCustom, calls=%fused_computation.22 | custom fusion | flops 245760 | bytes 787712 | tf_op jit(solution)/shard_map/scatter-add | solution.py:159
  188.4 2.3 %slice.24 = f32[1024,192]{1,0:T(8,128)} slice(f32[1025,192]{1,0:T(8,128)} %scatter_custom_fusion.2), slice={[0:1024], [0:192]} | slice | bytes 1572864 | tf_op jit(solution)/shard_map/slice | solution.py:159
  190.7 2.4 %copy.120 = f32[1024,192]{0,1:T(8,128)} copy(f32[1024,192]{1,0:T(8,128)} %slice.24) | data formatting | bytes 1572864
  193.1 1.3 multiply_bitcast_fusion
  194.6 0.6 fusion.46
  195.7 1.0 copy.117
  196.8 1.0 copy.116
  (69 shorter events, 3.4 us)
Async XLA Ops:
  7.2 50.6 %copy-start = (bf16[1024,1536]{1,0:T(8,128)(2,1)S(1)}, bf16[1024,1536]{1,0:T(8,128)(2,1)}, u32[]{:S(2)}) copy-start(bf16[1024,1536]{1,0:T(8,128)(2,1)} %param.19) | copy-start | bytes 9437188
  21.9 15.7 %all-to-all-start.1 = ((bf16[16,8,1536]{2,1,0:T(8,128)(2,1)}), bf16[16,8,1536]{2,1,0:T(8,128)(2,1)S(1)}, u32[]{:S(2)}, u32[]{:S(2)}) async-start(bf16[16,8,1536]{2,1,0:T(8,128)(2,1)} %param.13), calls=%async_computation.1 | async-start | bytes 786432 | tf_op jit(solution)/shard_map/all_to_all | solution.py:59
  25.4 43.5 %reduce-scatter.3.cloned.1.call-start = ((), (), s32[]{:S(2)}) async-start(), calls=%async_computation.7 | async-start | bytes 294912 | tf_op jit(solution)/shard_map/reduce_scatter | solution.py:78
  38.8 5.2 %copy-start.13 = (bf16[128,8]{0,1:T(8,128)(2,1)S(1)}, bf16[128,8]{0,1:T(8,128)(2,1)}, u32[]{:S(2)}) copy-start(bf16[128,8]{0,1:T(8,128)(2,1)} %param.16) | copy-start | bytes 6148
  44.0 6.4 %copy-start.9 = (f32[1024]{0:T(1024)S(1)}, f32[1024]{0:T(1024)}, u32[]{:S(2)}) copy-start(f32[1024]{0:T(1024)} %param.17) | copy-start | bytes 12292
  45.6 0.7 copy-start.7
  47.8 7.2 %copy-start.15 = (f32[16]{0:T(128)}, f32[16]{0:T(128)S(1)}, u32[]{:S(2)}) copy-start(f32[16]{0:T(128)S(1)} %broadcast_multiply_fusion.6) | copy-start | bytes 196
  49.1 5.9 %copy-start.16 = (f32[16]{0:T(128)}, f32[16]{0:T(128)S(1)}, u32[]{:S(2)}) copy-start(f32[16]{0:T(128)S(1)} %add_rsqrt_fusion.1) | copy-start | bytes 196
  50.3 8.7 %copy-start.3 = (f32[16,1024]{1,0:T(8,128)}, f32[16,1024]{1,0:T(8,128)S(1)}, u32[]{:S(2)}) copy-start(f32[16,1024]{1,0:T(8,128)S(1)} %copy.100) | copy-start | bytes 196612
  57.1 0.6 copy-start.2
  57.7 1.4 copy-start.8
  57.7 1.6 copy-start.12
  59.0 36.0 %reduce-scatter.5.cloned.1.call-start = ((), (), s32[]{:S(2)}) async-start(), calls=%async_computation.8 | async-start | bytes 98304 | tf_op jit(solution)/shard_map/reduce_scatter | solution.py:100
  72.1 0.7 copy-start.4
  101.4 4.3 %copy-start.14 = (bf16[128,8]{0,1:T(8,128)(2,1)S(1)}, bf16[128,8]{0,1:T(8,128)(2,1)}, u32[]{:S(2)}) copy-start(bf16[128,8]{0,1:T(8,128)(2,1)} %param.16) | copy-start | bytes 6148
  103.8 3.3 %copy-start.1 = (f32[16,192,128]{2,1,0:T(8,128)S(1)}, f32[16,192,128]{2,1,0:T(8,128)}, u32[]{:S(2)}) copy-start(f32[16,192,128]{2,1,0:T(8,128)} %fusion.12) | copy-start | bytes 4718596
  103.8 3.3 %copy-start.11 = (bf16[16,128]{1,0:T(8,128)(2,1)S(1)}, bf16[16,128]{1,0:T(8,128)(2,1)}, u32[]{:S(2)}) copy-start(bf16[16,128]{1,0:T(8,128)(2,1)} %param.21) | copy-start | bytes 12292
  108.8 3.0 %copy-start.6 = (s32[16,128]{0,1:T(8,128)S(1)}, s32[16,128]{0,1:T(8,128)}, u32[]{:S(2)}) copy-start(s32[16,128]{0,1:T(8,128)} %bitcast_bitcast_fusion.1) | copy-start | bytes 24580
  115.3 8.3 %copy-start.10 = (s32[16,8,8]{0,2,1:T(8,128)S(1)}, s32[16,8,8]{0,2,1:T(8,128)}, u32[]{:S(2)}) copy-start(s32[16,8,8]{0,2,1:T(8,128)} %param.14) | copy-start | bytes 12292
  117.7 24.6 %all-to-all-start.3 = ((f32[16,8,1536]{2,1,0:T(8,128)}), f32[16,8,1536]{2,1,0:T(8,128)}, u32[]{:S(2)}, u32[]{:S(2)}) async-start(f32[16,8,1536]{2,1,0:T(8,128)} %reshape.270), calls=%async_computation.5 | async-start | bytes 1572864 | tf_op jit(solution)/shard_map/all_to_all | solution.py:123
  142.3 14.7 %all-to-all-start.2 = ((f32[2,1,640]{2,1,0:T(1,128)}), f32[2,1,640]{2,1,0:T(1,128)S(1)}, u32[]{:S(2)}, u32[]{:S(2)}) async-start(f32[2,1,640]{2,1,0:T(1,128)} %all_to_all.36), calls=%async_computation.3 | async-start | bytes 10240 | tf_op jit(solution)/shard_map/all_to_all | solution.py:154
  157.0 18.2 %all-to-all-start.4 = ((f32[2,640,192]{1,2,0:T(8,128)}), f32[2,640,192]{1,2,0:T(8,128)}, u32[]{:S(2)}, u32[]{:S(2)}) async-start(f32[2,640,192]{1,2,0:T(8,128)} %copy.112), calls=%async_computation.6 | async-start | bytes 1966080 | tf_op jit(solution)/shard_map/all_to_all | solution.py:151
  193.1 1.5 copy-start.17
  193.1 2.1 %copy-start.5 = (f32[8,128,192]{1,2,0:T(8,128)S(1)}, f32[8,128,192]{1,2,0:T(8,128)}, u32[]{:S(2)}) copy-start(f32[8,128,192]{1,2,0:T(8,128)} %param.24) | copy-start | bytes 2359300
Sparse Core Ops, SparseCore 0:
  59.2 9.7 reduce-scatter.2
  84.2 10.8 reduce-scatter.4
where the time goes:
time: 206 us; the launch traced here: 205 us
  local copies, waits for them, and re-layouts  51.8 us (25%)
  waiting for transfers between devices  47.1 us (23%)
  matrix products  30.7 us (15%)
  blocking collectives  23.3 us (11%)
  other arithmetic  20.3 us (10%)
  starting transfers between devices  17.1 us (8%)
  between operations  14.4 us (7%)
    all_to_all x1, blocking collectives, body(): lax.all_to_all(index_local, 'col', split_axis=0, concat_axis=2, tiled=True)  13.6 us
    all_to_all x1, waiting for transfers between devices, body(): lax.all_to_all(list_grads.reshape(columns, slot_dev, uniq * width), 'col'...  12.1 us
    all_to_all x1, waiting for transfers between devices, body(): lax.all_to_all(bucket.reshape(owners, capacity, width), 'row', split_axis...  10.7 us
    scatter-add x1, other arithmetic, body(): jax.ops.segment_sum(got_rows.reshape(-1, width), segment, num_segments=sp...  10.5 us
    all_to_all x1, waiting for transfers between devices, body(): lax.all_to_all(uniq_rows, 'col', split_axis=0, concat_axis=1, tiled=True)  8.72 us
    reduce_scatter x1, waiting for transfers between devices, body(): lax.psum_scatter(jnp.dot(part_rows, w_down, preferred_element_type=jnp.fl...  8 us
    unnamed x43, local copies, waits for them, and re-layouts  7.56 us
    reduce_scatter x1, waiting for transfers between devices, body(): lax.psum_scatter(lax.dot_general(part_rows, w_up, (((1,), (1,)), ((), ())...  7.52 us
  transfers between devices with their start and end apart: 6, of which 5 were waited for; matrix products, arithmetic and copies ran while one was open for 14% of the time, Pallas kernels for 0%

commit v1 on v0

--- a/solution.py
+++ b/solution.py
@@ -52,9 +52,12 @@
     out_rows = w_res.shape[0]
     entry_iota = jnp.arange(uniq, dtype=jnp.int32)
     index_local = sample_idx.reshape(columns, samples, slot_dev)
-    index = lax.all_to_all(index_local, "col", split_axis=0, concat_axis=2, tiled=True).reshape(
-        samples, slots
-    )
+    index = jnp.concatenate(
+        lax.all_to_all(
+            jnp.stack(jnp.split(index_local, lax.axis_size("col"), axis=0)), "col", 0, 0
+        ),
+        axis=2,
+    ).reshape(samples, slots)
     picker = (index[:, :, None] == entry_iota).astype(jnp.bfloat16)
     moved = lax.all_to_all(uniq_rows, "col", split_axis=0, concat_axis=1, tiled=True)
     table = moved.reshape(slots, uniq, width)

time: 206 us -> 218 us (1.058)
  local copies, waits for them, and re-layouts: 51.8 us -> 63.1 us
    unnamed x43 -> x58, local copies, waits for them, and re-layouts: 7.56 us -> 19 us
  transfers between devices with their start and end apart: 6 -> 6, of which waited for: 5 -> 5; matrix products, arithmetic and copies ran while one was open for 14% -> 13% of each run, Pallas kernels for 0% -> 0%
where the time goes in v1:
time: 218 us; the launch traced here: 216 us
  local copies, waits for them, and re-layouts  63.1 us (29%)
  waiting for transfers between devices  47 us (22%)
  matrix products  30.7 us (14%)
  blocking collectives  23.4 us (11%)
  other arithmetic  20.3 us (9%)
  starting transfers between devices  17.1 us (8%)
  between operations  14.4 us (7%)
    unnamed x58, local copies, waits for them, and re-layouts  19 us
    all_to_all x1, blocking collectives, body(): lax.all_to_all(jnp.stack(jnp.split(index_local, lax.axis_size('col'), axi...  13.6 us
    all_to_all x1, waiting for transfers between devices, body(): lax.all_to_all(list_grads.reshape(columns, slot_dev, uniq * width), 'col'...  12.1 us
    all_to_all x1, waiting for transfers between devices, body(): lax.all_to_all(bucket.reshape(owners, capacity, width), 'row', split_axis...  10.6 us
    scatter-add x1, other arithmetic, body(): jax.ops.segment_sum(got_rows.reshape(-1, width), segment, num_segments=sp...  10.5 us
    all_to_all x1, waiting for transfers between devices, body(): lax.all_to_all(uniq_rows, 'col', split_axis=0, concat_axis=1, tiled=True)  8.72 us
    reduce_scatter x1, waiting for transfers between devices, body(): lax.psum_scatter(jnp.dot(part_rows, w_down, preferred_element_type=jnp.fl...  8 us
    reduce_scatter x1, waiting for transfers between devices, body(): lax.psum_scatter(lax.dot_general(part_rows, w_up, (((1,), (1,)), ((), ())...  7.49 us
  transfers between devices with their start and end apart: 6, of which 5 were waited for; matrix products, arithmetic and copies ran while one was open for 13% of the time, Pallas kernels for 0%

profile of v1, /device:TPU:0, one launch (start us, length us, event | category | flops | bytes accessed | tf_op | source)
XLA Modules:
  0.0 216.1 jit_solution(14316174603087046279)
XLA Ops:
  7.2 0.8 constant_dynamic-update-slice_fusion.15
  8.0 0.9 constant_dynamic-update-slice_fusion.14
  8.9 0.8 constant_dynamic-update-slice_fusion.13
  9.6 0.8 constant_dynamic-update-slice_fusion.12
  10.4 0.8 constant_dynamic-update-slice_fusion.11
  11.2 0.8 constant_dynamic-update-slice_fusion.10
  11.9 0.8 constant_dynamic-update-slice_fusion.9
  12.7 0.8 constant_dynamic-update-slice_fusion.8
  14.1 0.8 constant_dynamic-update-slice_fusion.6
  16.4 0.8 constant_dynamic-update-slice_fusion.3
  17.2 0.8 constant_dynamic-update-slice_fusion.2
  19.5 13.6 %all_to_all.36 = s32[16,1,128]{2,1,0:T(1,128)S(1)} all-to-all(s32[16,1,128]{2,1,0:T(1,128)S(1)} %reshape.348), channel_id=1, replica_groups=mesh['col'=16,'row'=2] {'col'}, dimensions={0} | all-to-all | bytes 16384 | tf_op jit(solution)/shard_map/all_to_all | solution.py:56
  33.1 3.6 %all-to-all-start.1 = ((bf16[16,8,1536]{2,1,0:T(8,128)(2,1)}), bf16[16,8,1536]{2,1,0:T(8,128)(2,1)S(1)}, u32[]{:S(2)}, u32[]{:S(2)}) async-start(bf16[16,8,1536]{2,1,0:T(8,128)(2,1)} %param.13), calls=%async_computation.1 | async-start | bytes 786432 | tf_op jit(solution)/shard_map/all_to_all | solution.py:62
  38.7 1.5 bitcast_bitcast_fusion.1
  40.1 8.7 %all-to-all-done.1 = bf16[16,8,1536]{2,1,0:T(8,128)(2,1)S(1)} async-done(((bf16[16,8,1536]{2,1,0:T(8,128)(2,1)}), bf16[16,8,1536]{2,1,0:T(8,128)(2,1)S(1)}, u32[]{:S(2)}, u32[]{:S(2)}) %all-to-all-start.1) | async-done | bytes 393248 | tf_op jit(solution)/shard_map/all_to_all | solution.py:62
  48.8 1.2 reshape.292
  50.0 2.6 %fusion = bf16[16,128,192]{2,0,1:T(8,128)(2,1)} fusion(bf16[128,8,192]{2,1,0:T(8,128)(2,1)} %reshape.292, s32[16,128]{0,1:T(8,128)} %bitcast_bitcast_fusion.1), kind=kOutput, calls=%fused_computation.7 | convolution fusion | flops 6701056 | bytes 1187840 | tf_op jit(solution)/shard_map/stl,tle->ste/dot_general | solution.py:64
  52.7 2.6 %copy.93 = bf16[16,128,192]{1,2,0:T(8,128)(2,1)} copy(bf16[16,128,192]{2,0,1:T(8,128)(2,1)} %fusion) | data formatting | bytes 1572864 | tf_op jit(solution)/shard_map/convert_element_type | solution.py:64
  55.3 1.6 convolution_convert_fusion.1
  57.5 1.5 fusion.47
  59.1 1.0 copy.94
  60.4 1.2 copy.95
  61.7 4.6 %all_gather.6 = bf16[32,1024]{1,0:T(8,128)(2,1)S(1)} all-gather(bf16[16,1024]{1,0:T(8,128)(2,1)S(1)} %multiply_convert_fusion.2), channel_id=1, replica_groups=mesh['col'=16,'row'=2] {'row'}, dimensions={0}, use_global_device_ids=true | all-gather | bytes 98304 | tf_op jit(solution)/shard_map/all_gather | solution.py:75
  66.3 2.1 fusion.48
  69.0 1.3 fusion.19
  70.6 1.6 convolution_bitcast_fusion.1
  72.2 8.0 %reduce-scatter.3.cloned.1.call-done = f32[16,1536]{1,0:T(8,128)} async-done(((f32[32,1536]{1,0:T(8,128)}), f32[16,1536]{1,0:T(8,128)}) %reduce-scatter.3.cloned.1.call-update) | async-done | bytes 98320 | tf_op jit(solution)/shard_map/reduce_scatter | solution.py:81
  80.2 1.0 reshape.294
  81.5 0.9 fusion.9
  82.5 0.9 subtract_multiply_fusion
  84.7 1.6 convert_element_type.72
  86.3 5.2 %all_gather.7 = bf16[32,1536]{1,0:T(8,128)(2,1)} all-gather(bf16[16,1536]{1,0:T(8,128)(2,1)} %convert_element_type.72), channel_id=1, replica_groups=mesh['col'=16,'row'=2] {'row'}, dimensions={0}, use_global_device_ids=true | all-gather | bytes 147456 | tf_op jit(solution)/shard_map/all_gather | solution.py:96
  91.5 4.0 %convolution_convert_fusion.2 = bf16[32,1024]{1,0:T(8,128)(2,1)} fusion(bf16[1024,1024]{1,0:T(8,128)(2,1)} %param.18, bf16[32,1536]{1,0:T(8,128)(2,1)} %all_gather.7, bf16[1024,1536]{1,0:T(8,128)(2,1)S(1)} %copy-done, f32[32,1024]{1,0:T(8,128)} %copy-done.2), kind=kOutput, calls=%fused_computation.15 | convolution fusion | flops 168099840 | bytes 5537792 | tf_op jit(solution)/shard_map/dot_general | solution.py:104
  95.5 3.5 %fusion.12 = f32[16,192,128]{2,1,0:T(8,128)} fusion(f32[16,16,192]{2,1,0:T(8,128)} %copy-done.4, bf16[8,128]{1,0:T(8,128)(2,1)} %param.20), kind=kOutput, calls=%fused_computation.36 | convolution fusion | flops 37748736 | bytes 1705984 | tf_op jit(solution)/shard_map/lt,sle->ste/dot_general | solution.py:119
  99.0 7.5 %reduce-scatter.5.cloned.1.call-done = bf16[16,1024]{1,0:T(8,128)(2,1)} async-done(((bf16[32,1024]{1,0:T(8,128)(2,1)}), bf16[16,1024]{1,0:T(8,128)(2,1)}) %reduce-scatter.5.cloned.1.call-update) | async-done | bytes 32784 | tf_op jit(solution)/shard_map/reduce_scatter | solution.py:103
  106.5 1.0 fusion.20
  107.6 1.6 subtract_multiply_fusion.2
  109.2 1.8 copy.102
  111.0 1.8 copy.103
  112.8 2.4 %fusion.50 = f32[16,192,8]{1,2,0:T(8,128)S(1)} fusion(bf16[16,128,192]{1,2,0:T(8,128)(2,1)} %copy.93, f32[16,128,8]{1,2,0:T(8,128)} %copy.103), kind=kOutput, calls=%fused_computation.131 | convolution fusion | flops 37748736 | bytes 950272 | tf_op jit(solution)/shard_map/ste,stk->sek/dot_general | solution.py:113
  115.3 1.9 fusion.49
  117.2 1.4 fusion.41
  118.6 1.6 bitcast_add_fusion
  120.2 3.0 %copy.106 = f32[16,128,192]{2,0,1:T(8,128)} copy(f32[16,128,192]{1,2,0:T(8,128)} %bitcast_add_fusion) | data formatting | bytes 3145728 | tf_op jit(solution)/shard_map/add | solution.py:122
  123.3 3.5 %fusion.8 = f32[128,8,192]{2,1,0:T(8,128)} fusion(f32[16,128,192]{2,0,1:T(8,128)} %copy.106, s32[16,128]{0,1:T(8,128)S(1)} %copy-done.6), kind=kOutput, calls=%fused_computation.25 | convolution fusion | flops 37765120 | bytes 2367488 | tf_op jit(solution)/shard_map/stl,ste->tle/dot_general | solution.py:125
  126.7 2.4 %reshape.302 = f32[16,8,1536]{2,1,0:T(8,128)} reshape(f32[128,8,192]{2,1,0:T(8,128)} %fusion.8) | data formatting | bytes 1572864 | tf_op jit(solution)/shard_map/reshape | solution.py:127
  129.2 5.7 %all-to-all-start.3 = ((f32[16,8,1536]{2,1,0:T(8,128)}), f32[16,8,1536]{2,1,0:T(8,128)}, u32[]{:S(2)}, u32[]{:S(2)}) async-start(f32[16,8,1536]{2,1,0:T(8,128)} %reshape.302), calls=%async_computation.5 | async-start | bytes 1572864 | tf_op jit(solution)/shard_map/all_to_all | solution.py:126
  136.5 4.3 %scatter_custom_fusion = f32[1280]{0:T(1024)S(1)} fusion(s32[1024]{0:T(1024)S(1)} %bitcast.138, f32[1024]{0:T(1024)S(1)} %get-tuple-element.34, f32[]{:T(128)} %constant.65.clone.1), kind=kCustom, calls=%fused_computation.107 | custom fusion | bytes 5124 | tf_op jit(solution)/shard_map/scatter | solution.py:151
  141.4 12.1 %all-to-all-done.3 = f32[16,8,1536]{2,1,0:T(8,128)} async-done(((f32[16,8,1536]{2,1,0:T(8,128)}), f32[16,8,1536]{2,1,0:T(8,128)}, u32[]{:S(2)}, u32[]{:S(2)}) %all-to-all-start.3) | async-done | bytes 786464 | tf_op jit(solution)/shard_map/all_to_all | solution.py:126
  153.6 3.2 %all-to-all-start.2 = ((f32[2,1,640]{2,1,0:T(1,128)}), f32[2,1,640]{2,1,0:T(1,128)S(1)}, u32[]{:S(2)}, u32[]{:S(2)}) async-start(f32[2,1,640]{2,1,0:T(1,128)} %all_to_all.26), calls=%async_computation.3 | async-start | bytes 10240 | tf_op jit(solution)/shard_map/all_to_all | solution.py:157
  156.8 2.4 %reshape.318 = f32[1024,192]{1,0:T(8,128)} reshape(f32[16,8,1536]{2,1,0:T(8,128)} %all-to-all-done.3) | data formatting | bytes 1572864 | tf_op jit(solution)/shard_map/reshape | solution.py:133
  159.2 6.4 %scatter_custom_fusion.1 = f32[1280,192]{1,0:T(8,128)} fusion(s32[1024]{0:T(1024)S(1)} %bitcast.139, f32[1024,192]{1,0:T(8,128)} %reshape.318, f32[]{:T(128)} %constant.59.clone.1), kind=kCustom, calls=%fused_computation.20 | custom fusion | bytes 983552 | tf_op jit(solution)/shard_map/scatter | solution.py:147
  165.6 2.7 %copy.107 = f32[2,640,192]{1,2,0:T(8,128)} copy(f32[2,640,192]{2,1,0:T(8,128)} %bitcast.131) | data formatting | bytes 1966080 | tf_op jit(solution)/shard_map/reshape | solution.py:155
  168.3 4.6 %all-to-all-start.4 = ((f32[2,640,192]{1,2,0:T(8,128)}), f32[2,640,192]{1,2,0:T(8,128)}, u32[]{:S(2)}, u32[]{:S(2)}) async-start(f32[2,640,192]{1,2,0:T(8,128)} %copy.107), calls=%async_computation.6 | async-start | bytes 1966080 | tf_op jit(solution)/shard_map/all_to_all | solution.py:154
  173.6 1.7 fusion.2
  175.2 0.8 convert_element_type.67
  176.0 10.6 %all-to-all-done.4 = f32[2,640,192]{1,2,0:T(8,128)} async-done(((f32[2,640,192]{1,2,0:T(8,128)}), f32[2,640,192]{1,2,0:T(8,128)}, u32[]{:S(2)}, u32[]{:S(2)}) %all-to-all-start.4) | async-done | bytes 983072 | tf_op jit(solution)/shard_map/all_to_all | solution.py:154
  186.7 2.7 %copy.113 = f32[2,640,192]{2,1,0:T(8,128)} copy(f32[2,640,192]{1,2,0:T(8,128)} %all-to-all-done.4) | data formatting | bytes 1966080 | tf_op jit(solution)/shard_map/reshape | solution.py:162
  189.3 10.5 %scatter_custom_fusion.2 = f32[1025,192]{1,0:T(8,128)} fusion(s32[1280]{0:T(1024)} %fusion.28, f32[1280,192]{1,0:T(8,128)} %bitcast.134, f32[]{:T(128)} %constant.59.clone.1), kind=kCustom, calls=%fused_computation.22 | custom fusion | flops 245760 | bytes 787712 | tf_op jit(solution)/shard_map/scatter-add | solution.py:162
  199.8 2.3 %slice.40 = f32[1024,192]{1,0:T(8,128)} slice(f32[1025,192]{1,0:T(8,128)} %scatter_custom_fusion.2), slice={[0:1024], [0:192]} | slice | bytes 1572864 | tf_op jit(solution)/shard_map/slice | solution.py:162
  202.1 2.4 %copy.115 = f32[1024,192]{0,1:T(8,128)} copy(f32[1024,192]{1,0:T(8,128)} %slice.40) | data formatting | bytes 1572864
  204.5 1.3 multiply_bitcast_fusion
  207.2 1.0 copy.112
  208.2 1.0 copy.111
  (83 shorter events, 13.5 us)
Async XLA Ops:
  7.2 61.8 %copy-start = (bf16[1024,1536]{1,0:T(8,128)(2,1)S(1)}, bf16[1024,1536]{1,0:T(8,128)(2,1)}, u32[]{:S(2)}) copy-start(bf16[1024,1536]{1,0:T(8,128)(2,1)} %param.19) | copy-start | bytes 9437188
  33.1 15.7 %all-to-all-start.1 = ((bf16[16,8,1536]{2,1,0:T(8,128)(2,1)}), bf16[16,8,1536]{2,1,0:T(8,128)(2,1)S(1)}, u32[]{:S(2)}, u32[]{:S(2)}) async-start(bf16[16,8,1536]{2,1,0:T(8,128)(2,1)} %param.13), calls=%async_computation.1 | async-start | bytes 786432 | tf_op jit(solution)/shard_map/all_to_all | solution.py:62
  36.7 43.5 %reduce-scatter.3.cloned.1.call-start = ((), (), s32[]{:S(2)}) async-start(), calls=%async_computation.7 | async-start | bytes 294912 | tf_op jit(solution)/shard_map/reduce_scatter | solution.py:81
  50.0 5.2 %copy-start.13 = (bf16[128,8]{0,1:T(8,128)(2,1)S(1)}, bf16[128,8]{0,1:T(8,128)(2,1)}, u32[]{:S(2)}) copy-start(bf16[128,8]{0,1:T(8,128)(2,1)} %param.16) | copy-start | bytes 6148
  55.3 6.4 %copy-start.9 = (f32[1024]{0:T(1024)S(1)}, f32[1024]{0:T(1024)}, u32[]{:S(2)}) copy-start(f32[1024]{0:T(1024)} %param.17) | copy-start | bytes 12292
  56.9 0.7 copy-start.7
  59.1 7.2 %copy-start.15 = (f32[16]{0:T(128)}, f32[16]{0:T(128)S(1)}, u32[]{:S(2)}) copy-start(f32[16]{0:T(128)S(1)} %broadcast_multiply_fusion.6) | copy-start | bytes 196
  60.4 5.9 %copy-start.16 = (f32[16]{0:T(128)}, f32[16]{0:T(128)S(1)}, u32[]{:S(2)}) copy-start(f32[16]{0:T(128)S(1)} %add_rsqrt_fusion.1) | copy-start | bytes 196
  61.6 8.7 %copy-start.3 = (f32[16,1024]{1,0:T(8,128)}, f32[16,1024]{1,0:T(8,128)S(1)}, u32[]{:S(2)}) copy-start(f32[16,1024]{1,0:T(8,128)S(1)} %copy.95) | copy-start | bytes 196612
  68.4 0.6 copy-start.2
  69.0 1.4 copy-start.8
  69.0 1.6 copy-start.12
  70.3 36.2 %reduce-scatter.5.cloned.1.call-start = ((), (), s32[]{:S(2)}) async-start(), calls=%async_computation.8 | async-start | bytes 98304 | tf_op jit(solution)/shard_map/reduce_scatter | solution.py:103
  83.3 0.7 copy-start.4
  112.8 4.3 %copy-start.14 = (bf16[128,8]{0,1:T(8,128)(2,1)S(1)}, bf16[128,8]{0,1:T(8,128)(2,1)}, u32[]{:S(2)}) copy-start(bf16[128,8]{0,1:T(8,128)(2,1)} %param.16) | copy-start | bytes 6148
  115.3 3.3 %copy-start.1 = (f32[16,192,128]{2,1,0:T(8,128)S(1)}, f32[16,192,128]{2,1,0:T(8,128)}, u32[]{:S(2)}) copy-start(f32[16,192,128]{2,1,0:T(8,128)} %fusion.12) | copy-start | bytes 4718596
  115.3 3.3 %copy-start.11 = (bf16[16,128]{1,0:T(8,128)(2,1)S(1)}, bf16[16,128]{1,0:T(8,128)(2,1)}, u32[]{:S(2)}) copy-start(bf16[16,128]{1,0:T(8,128)(2,1)} %param.21) | copy-start | bytes 12292
  120.2 3.0 %copy-start.6 = (s32[16,128]{0,1:T(8,128)S(1)}, s32[16,128]{0,1:T(8,128)}, u32[]{:S(2)}) copy-start(s32[16,128]{0,1:T(8,128)} %bitcast_bitcast_fusion.1) | copy-start | bytes 24580
  126.7 8.1 %copy-start.10 = (s32[16,8,8]{0,2,1:T(8,128)S(1)}, s32[16,8,8]{0,2,1:T(8,128)}, u32[]{:S(2)}) copy-start(s32[16,8,8]{0,2,1:T(8,128)} %param.14) | copy-start | bytes 12292
  129.2 24.4 %all-to-all-start.3 = ((f32[16,8,1536]{2,1,0:T(8,128)}), f32[16,8,1536]{2,1,0:T(8,128)}, u32[]{:S(2)}, u32[]{:S(2)}) async-start(f32[16,8,1536]{2,1,0:T(8,128)} %reshape.302), calls=%async_computation.5 | async-start | bytes 1572864 | tf_op jit(solution)/shard_map/all_to_all | solution.py:126
  153.6 14.7 %all-to-all-start.2 = ((f32[2,1,640]{2,1,0:T(1,128)}), f32[2,1,640]{2,1,0:T(1,128)S(1)}, u32[]{:S(2)}, u32[]{:S(2)}) async-start(f32[2,1,640]{2,1,0:T(1,128)} %all_to_all.26), calls=%async_computation.3 | async-start | bytes 10240 | tf_op jit(solution)/shard_map/all_to_all | solution.py:157
  168.3 18.4 %all-to-all-start.4 = ((f32[2,640,192]{1,2,0:T(8,128)}), f32[2,640,192]{1,2,0:T(8,128)}, u32[]{:S(2)}, u32[]{:S(2)}) async-start(f32[2,640,192]{1,2,0:T(8,128)} %copy.107), calls=%async_computation.6 | async-start | bytes 1966080 | tf_op jit(solution)/shard_map/all_to_all | solution.py:154
  204.5 1.5 copy-start.17
  204.5 2.1 copy-start.5
Sparse Core Ops, SparseCore 0:
  70.4 9.7 reduce-scatter.2
  95.7 10.8 reduce-scatter.4
